TPU v7x, 256 devices: a whole 4x4x8 slice. The times are simulated.
256 devices in a mesh: own: 64 (over z, x, core), grp: 4 (over y).
Axes of the slice: x: 4, y: 4, z: 8, core: 2. Of those that a mesh axis runs over, the one named last changes fastest.
Arguments:
- panel: float32 [64, 4, 768, 768], P('own', 'grp'), may hold values from -6 to 6
- diag_inverse: float32 [64, 768, 768], P('own', 'grp'), as said below
- ancestor: float32 [64, 4, 768, 768], P('own', 'grp'), may hold values from -6 to 6
- live_blocks: int32 [64], P('own'), may hold values from 1 to 4
- pair_first: int32 [64, 4, 7], P('own', 'grp'), may hold values from 0 to 3
- pair_second: int32 [64, 4, 7], P('own', 'grp'), may hold values from 0 to 3
- pair_offset: int32 [64, 4, 7], P('own', 'grp'), may hold values from 0 to 4
Outputs:
- solved: float32 [64, 4, 768, 768], P('own', 'grp')
- updated: float32 [64, 4, 768, 768], P('own', 'grp')
Inputs may be any that keep to these rules, and one draw needn't show every extreme that they name: diag_inverse[s] is upper triangular with a positive diagonal.
All inputs are finite; a program needn't handle non-finite values.
Results may differ from a plain program's by a relative error of at most 0.0001.
Values sent between devices are 32-bit elements; how exact they have to be, the bound alone decides.
A program may use at most 128 MiB of HBM per device.

v0:
```python
import jax
import jax.numpy as jnp
from jax import lax
from jax.sharding import PartitionSpec as P

REACH = 5


def joined_along(parts, dim):
    parts = jnp.moveaxis(parts, 0, dim)
    lengths = parts.shape
    return parts.reshape(*lengths[:dim], lengths[dim] * lengths[dim + 1], *lengths[dim + 2 :])


def copy_for_each(array, axis):
    copies = jnp.broadcast_to(array, (lax.axis_size(axis), *array.shape))
    return lax.all_to_all(copies, axis, split_axis=0, concat_axis=0, tiled=True)


def gather_directly(array, axis, dim):
    return joined_along(copy_for_each(array, axis), dim)


def passed_along(array, axis, by):
    size = lax.axis_size(axis)
    return lax.ppermute(array, axis, [(i, (i + by) % size) for i in range(size)])


def shards(panel, diag_inverse, ancestor, live_blocks, pair_first, pair_second, pair_offset):
    group_index = lax.axis_index("grp")
    factor = gather_directly(diag_inverse, "grp", 1)
    alive = (group_index < live_blocks[0]).astype(jnp.float32)
    solved = alive * jnp.dot(panel[0, 0], factor[0], precision=lax.Precision.HIGHEST)
    column = lax.all_gather(solved[None], "grp", axis=0, tiled=True)
    first = column[pair_first[0, 0]]
    second = column[pair_second[0, 0]]
    terms = jnp.einsum("pij,pkj->pik", first, second, precision=lax.Precision.HIGHEST)
    distances = jnp.arange(REACH, dtype=jnp.int32)
    weights = (pair_offset[0, 0][None, :] == distances[:, None]).astype(jnp.float32)
    outgoing = jnp.einsum("dp,pik->dik", weights, terms, precision=lax.Precision.HIGHEST)
    received = outgoing[0]
    for distance in range(1, REACH):
        received = received + passed_along(outgoing[distance], "own", distance)
    updated = ancestor[0, 0] - received
    return (solved[None, None], updated[None, None])


def solution(mesh):
    placed = (
        P("own", "grp", None, None),
        P("own", "grp", None),
        P("own", "grp", None, None),
        P("own"),
        P("own", "grp", None),
        P("own", "grp", None),
        P("own", "grp", None),
    )
    return jax.shard_map(
        shards,
        mesh=mesh,
        in_specs=placed,
        out_specs=(P("own", "grp", None, None), P("own", "grp", None, None)),
        check_vma=False,
    )
```

profile of v0, /device:TPU:1, one launch (start us, length us, event | category | flops | bytes accessed | tf_op | source)
XLA Modules:
  0.0 477.7 jit_solution(4008402591965512278)
XLA Ops:
  7.2 0.0 copy-start
  7.2 2.8 broadcast_in_dim.15
  10.0 5.0 %all-to-all-start = ((f32[4,1,192,768]{3,2,1,0:T(8,128)}), f32[4,1,192,768]{3,2,1,0:T(8,128)}, u32[]{:S(2)}, u32[]{:S(2)}) async-start(f32[4,1,192,768]{3,2,1,0:T(8,128)} %broadcast_in_dim.15), calls=%async_computation | async-start | bytes 4718592 | tf_op jit(solution)/shard_map/all_to_all | solution.py:17
  15.0 0.0 all-gather.3.cloned.1.call-start
  15.7 26.4 %all-to-all-done = f32[4,1,192,768]{3,2,1,0:T(8,128)} async-done(((f32[4,1,192,768]{3,2,1,0:T(8,128)}), f32[4,1,192,768]{3,2,1,0:T(8,128)}, u32[]{:S(2)}, u32[]{:S(2)}) %all-to-all-start) | async-done | bytes 2359328 | tf_op jit(solution)/shard_map/all_to_all | solution.py:17
  42.1 0.0 copy-done
  42.1 8.9 %fusion.10 = f32[768,768]{1,0:T(8,128)} fusion(f32[768,768]{1,0:T(8,128)} %bitcast.3, f32[1,1,768,768]{3,2,1,0:T(8,128)S(1)} %copy-done, f32[]{:T(128)S(6)} %convert_element_type.4), kind=kOutput, calls=%fused_computation.17 | convolution fusion | flops 5436407808 | bytes 7077892 | tf_op jit(solution)/shard_map/dot_general | solution.py:33
  51.0 0.0 copy-start.5
  51.0 0.0 copy-start.6
  51.0 0.0 all-gather.3.cloned.1.call-update
  51.0 0.6 copy-done.5
  51.6 0.0 copy-done.6
  51.7 97.7 %all-gather.3.cloned.1.call-done = f32[3072,768]{1,0:T(8,128)} async-done(((f32[768,768]{1,0:T(8,128)}), f32[3072,768]{1,0:T(8,128)}) %all-gather.3.cloned.1.call-update) | async-done | bytes 9437200 | tf_op jit(solution)/shard_map/all_gather | solution.py:34
  149.4 11.8 %gather_fusion.1 = f32[7,768,768]{2,1,0:T(8,128)} fusion(f32[4,768,768]{2,1,0:T(8,128)} %bitcast.56, s32[1024]{0:T(1024)S(1)} %pad_clamp_fusion), kind=kCustom, calls=%fused_computation.1 | custom fusion | bytes 33030172 | tf_op jit(solution)/shard_map/gather | solution.py:36
  161.2 11.8 %gather_fusion = f32[7,768,768]{2,1,0:T(8,128)} fusion(f32[4,768,768]{2,1,0:T(8,128)} %bitcast.57, s32[1024]{0:T(1024)S(1)} %pad_clamp_fusion.1), kind=kCustom, calls=%fused_computation | custom fusion | bytes 33030172 | tf_op jit(solution)/shard_map/gather | solution.py:35
  173.0 0.0 copy-start.4
  173.0 44.7 %fusion.19 = f32[7,768,768]{2,1,0:T(8,128)} fusion(f32[7,768,768]{2,1,0:T(8,128)} %gather_fusion, f32[7,768,768]{2,1,0:T(8,128)} %gather_fusion.1), kind=kOutput, calls=%fused_computation.28 | convolution fusion | flops 38050725888 | bytes 49545216 | tf_op jit(solution)/shard_map/pij,pkj->pik/dot_general | solution.py:37
  217.7 0.0 copy-done.4
  217.7 27.1 %fusion = f32[5,768,768]{2,0,1:T(8,128)} fusion(f32[7,768,768]{2,1,0:T(8,128)} %fusion.19, s32[7]{0:T(128)S(1)} %bitcast.64), kind=kOutput, calls=%fused_computation.2 | convolution fusion | flops 247726112 | bytes 28311580 | tf_op jit(solution)/shard_map/dp,pik->dik/dot_general | solution.py:40
  244.8 39.0 %fusion.18 = (f32[1,768,768]{2,0,1:T(1,128)}, f32[1,768,768]{2,0,1:T(1,128)S(1)}, f32[1,768,768]{2,0,1:T(1,128)S(1)}, f32[1,768,768]{2,0,1:T(1,128)S(1)}, f32[1,768,768]{2,0,1:T(1,128)S(1)}) fusion(f32[5,768,768]{2,0,1:T(8,128)} %fusion), kind=kLoop, calls=%fused_computation.27 | loop fusion | bytes 23592960 | tf_op jit(solution)/shard_map/slice | solution.py:41
  283.9 0.2 copy.39
  284.0 0.2 copy.40
  284.2 0.2 copy.41
  284.4 0.0 copy-start.2
  284.4 0.0 copy-start.3
  284.4 0.2 copy.38
  284.5 3.4 collective-permute-start.2
  287.9 0.8 collective-permute-start.3
  288.7 0.9 collective-permute-start
  289.6 0.6 collective-permute-start.1
  290.2 54.1 %collective-permute-done.2 = f32[768,768]{1,0:T(8,128)S(1)} collective-permute-done((f32[768,768]{1,0:T(8,128)S(1)}, f32[768,768]{1,0:T(8,128)S(1)}, u32[]{:S(2)}, u32[]{:S(2)}) %collective-permute-start.2) | collective-permute-done | bytes 2359328 | tf_op jit(solution)/shard_map/ppermute | solution.py:26
  344.3 47.8 %collective-permute-done.3 = f32[768,768]{1,0:T(8,128)S(1)} collective-permute-done((f32[768,768]{1,0:T(8,128)S(1)}, f32[768,768]{1,0:T(8,128)S(1)}, u32[]{:S(2)}, u32[]{:S(2)}) %collective-permute-start.3) | collective-permute-done | bytes 2359328 | tf_op jit(solution)/shard_map/ppermute | solution.py:26
  392.1 46.4 %collective-permute-done = f32[768,768]{1,0:T(8,128)S(1)} collective-permute-done((f32[768,768]{1,0:T(8,128)S(1)}, f32[768,768]{1,0:T(8,128)S(1)}, u32[]{:S(2)}, u32[]{:S(2)}) %collective-permute-start) | collective-permute-done | bytes 2359328 | tf_op jit(solution)/shard_map/ppermute | solution.py:26
  438.5 30.0 %collective-permute-done.1 = f32[768,768]{1,0:T(8,128)S(1)} collective-permute-done((f32[768,768]{1,0:T(8,128)S(1)}, f32[768,768]{1,0:T(8,128)S(1)}, u32[]{:S(2)}, u32[]{:S(2)}) %collective-permute-start.1) | collective-permute-done | bytes 2359328 | tf_op jit(solution)/shard_map/ppermute | solution.py:26
  468.5 0.0 copy-done.2
  468.5 0.0 copy-done.3
  468.5 0.0 copy-start.1
  468.5 2.3 fusion.7
  470.8 0.0 copy-done.1
  (4 shorter events, 0.0 us)
Async XLA Ops:
  7.2 34.9 %copy-start = (f32[1,1,768,768]{3,2,1,0:T(8,128)S(1)}, f32[1,1,768,768]{3,2,1,0:T(8,128)}, u32[]{:S(2)}) copy-start(f32[1,1,768,768]{3,2,1,0:T(8,128)} %param.7) | copy-start | bytes 7077892
  10.0 32.1 %all-to-all-start = ((f32[4,1,192,768]{3,2,1,0:T(8,128)}), f32[4,1,192,768]{3,2,1,0:T(8,128)}, u32[]{:S(2)}, u32[]{:S(2)}) async-start(f32[4,1,192,768]{3,2,1,0:T(8,128)} %broadcast_in_dim.15), calls=%async_computation | async-start | bytes 4718592 | tf_op jit(solution)/shard_map/all_to_all | solution.py:17
  15.0 134.4 %all-gather.3.cloned.1.call-start = ((), (), s32[]{:S(2)}) async-start(), calls=%async_computation.1 | async-start | bytes 11796480 | tf_op jit(solution)/shard_map/all_gather | solution.py:34
  51.0 0.7 copy-start.5
  51.0 0.7 copy-start.6
  173.0 44.7 %copy-start.4 = (s32[1,1,7]{2,1,0:T(1,128)S(1)}, s32[1,1,7]{2,1,0:T(1,128)}, u32[]{:S(2)}) copy-start(s32[1,1,7]{2,1,0:T(1,128)} %param.13) | copy-start | bytes 88
  284.4 184.1 %copy-start.2 = (f32[1,768,768]{2,0,1:T(1,128)S(1)}, f32[1,768,768]{2,0,1:T(1,128)}, u32[]{:S(2)}) copy-start(f32[1,768,768]{2,0,1:T(1,128)} %get-tuple-element.2) | copy-start | bytes 7077892
  284.4 184.1 %copy-start.3 = (f32[1,1,768,768]{3,2,1,0:T(8,128)S(1)}, f32[1,1,768,768]{3,2,1,0:T(8,128)}, u32[]{:S(2)}) copy-start(f32[1,1,768,768]{3,2,1,0:T(8,128)} %param.9) | copy-start | bytes 7077892
  284.5 59.7 %collective-permute-start.2 = (f32[768,768]{1,0:T(8,128)S(1)}, f32[768,768]{1,0:T(8,128)S(1)}, u32[]{:S(2)}, u32[]{:S(2)}) collective-permute-start(f32[768,768]{1,0:T(8,128)S(1)} %bitcast.62), channel_id=1, source_target_pairs={{0,12},{4,16},{8,20},{12,24},{16,28},{20,32},{24,36},{28,40},{32,4... | collective-permute-start | bytes 7077896 | tf_op jit(solution)/shard_map/ppermute | solution.py:26
  287.9 104.2 %collective-permute-start.3 = (f32[768,768]{1,0:T(8,128)S(1)}, f32[768,768]{1,0:T(8,128)S(1)}, u32[]{:S(2)}, u32[]{:S(2)}) collective-permute-start(f32[768,768]{1,0:T(8,128)S(1)} %bitcast.61), channel_id=1, source_target_pairs={{0,16},{4,20},{8,24},{12,28},{16,32},{20,36},{24,40},{28,44},{32,4... | collective-permute-start | bytes 7077896 | tf_op jit(solution)/shard_map/ppermute | solution.py:26
  288.7 149.8 %collective-permute-start = (f32[768,768]{1,0:T(8,128)S(1)}, f32[768,768]{1,0:T(8,128)S(1)}, u32[]{:S(2)}, u32[]{:S(2)}) collective-permute-start(f32[768,768]{1,0:T(8,128)S(1)} %bitcast.60), channel_id=1, source_target_pairs={{0,4},{4,8},{8,12},{12,16},{16,20},{20,24},{24,28},{28,32},{32,36}... | collective-permute-start | bytes 7077896 | tf_op jit(solution)/shard_map/ppermute | solution.py:26
  289.6 178.9 %collective-permute-start.1 = (f32[768,768]{1,0:T(8,128)S(1)}, f32[768,768]{1,0:T(8,128)S(1)}, u32[]{:S(2)}, u32[]{:S(2)}) collective-permute-start(f32[768,768]{1,0:T(8,128)S(1)} %bitcast.59), channel_id=1, source_target_pairs={{0,8},{4,12},{8,16},{12,20},{16,24},{20,28},{24,32},{28,36},{32,40... | collective-permute-start | bytes 7077896 | tf_op jit(solution)/shard_map/ppermute | solution.py:26
  468.5 2.3 copy-start.1
Sparse Core Ops, SparseCore 0:
  51.1 98.2 all-gather.2
where the time goes:
time: 481 us; the launch traced here: 478 us
  waiting for transfers between devices  302 us (63%)
  matrix products  80.8 us (17%)
  local copies, waits for them, and re-layouts  66.7 us (14%)
  between operations  14.8 us (3%)
  starting transfers between devices  10.7 us (2%)
    ppermute x4, waiting for transfers between devices, passed_along(): lax.ppermute(array, axis, [(i, (i + by) % size) for i in range(size)])  178 us
    all_gather x1, waiting for transfers between devices, shards(): column = lax.all_gather(solved[None], 'grp', axis=0, tiled=True)  97.7 us
    dot_general x1, matrix products, shards(): jnp.einsum('pij,pkj->pik', first, second, precision=lax.Precision.HIGHEST)  44.7 us
    slice x1, local copies, waits for them, and re-layouts, shards(): received = outgoing[0]  39 us
    dot_general x1, matrix products, shards(): jnp.einsum('dp,pik->dik', weights, terms, precision=lax.Precision.HIGHEST)  27.1 us
    all_to_all x1, waiting for transfers between devices, copy_for_each(): return lax.all_to_all(copies, axis, split_axis=0, concat_axis=0, tiled=True)  26.4 us
    gather x1, local copies, waits for them, and re-layouts, shards(): second = column[pair_second[0, 0]]  11.8 us
    gather x1, local copies, waits for them, and re-layouts, shards(): first = column[pair_first[0, 0]]  11.8 us
  transfers between devices with their start and end apart: 6, of which 6 were waited for; matrix products, arithmetic and copies ran while one was open for 0% of the time, Pallas kernels for 0%

commit v1 on v0

v1 whole, which is shorter than its diff:
```python
import jax
import jax.numpy as jnp
from jax import lax
from jax.experimental import pallas as pl
from jax.experimental.pallas import tpu as pltpu
from jax.sharding import PartitionSpec as P

MESH = pl.DeviceIdType.MESH
B = 768
PAIRS = 7
R = 128
C = B // R
TILES = C * C
SLAB = B // 4
GROUPS = ((0, 128, 1), (128, 256, 2), (384, 128, 3), (512, 256, 4))
NT = (((1,), (1,)), ((), ()))


def split(x):
    hi = x.astype(jnp.bfloat16)
    lo = (x - hi.astype(jnp.float32)).astype(jnp.bfloat16)
    return hi, lo


def kernel(
    live, first, second, offset, panel, diag, anc,
    solved_out, updated_out,
    factor, fac_hi, fac_lo, rows, solved, gath, halves, out, part, xin, base, upd, terms,
    local_sem, fac_send, fac_recv, near_send, near_recv, fwd_send, fwd_recv,
    part_send, part_recv, one_send, one_recv, two_send, two_recv,
):
    own = lax.axis_index("own")
    grp = lax.axis_index("grp")
    core = lax.rem(own, 2)

    def dev(by_own, by_grp):
        return (lax.rem(own + by_own + 64, 64), lax.rem(grp + by_grp + 4, 4))

    partner = (own + 1 - 2 * core, grp)
    up, down, across = dev(0, 1), dev(0, -1), dev(0, 2)

    load_rows = pltpu.make_async_copy(panel.at[0, 0], rows, local_sem.at[0])
    load_base = pltpu.make_async_copy(anc.at[0, 0], base, local_sem.at[1])
    load_rows.start()
    load_base.start()
    barrier = pltpu.get_barrier_semaphore()
    peers = (up, down, across, partner, dev(2, 0), dev(-2, 0), dev(4, 0), dev(-4, 0))
    for peer in peers:
        pl.semaphore_signal(barrier, 1, device_id=peer, device_id_type=MESH)
    pl.semaphore_wait(barrier, len(peers))

    def slab_copy(which, group, source_slab, target):
        start, width, _ = GROUPS[group]
        place = factor.at[pl.ds(pl.multiple_of(source_slab * SLAB, SLAB), SLAB), pl.ds(start, width)]
        return pltpu.make_async_remote_copy(
            diag.at[0, :, pl.ds(start, width)], place,
            fac_send.at[which, group], fac_recv.at[which, group],
            device_id=target, device_id_type=MESH,
        )

    for group in range(4):
        @pl.when(grp < GROUPS[group][2])
        def _():
            for which, target in enumerate((up, across, down)):
                slab_copy(which, group, grp, target).start()

    load_slab = pltpu.make_async_copy(
        diag.at[0], factor.at[pl.ds(pl.multiple_of(grp * SLAB, SLAB), SLAB)], local_sem.at[2]
    )
    load_slab.start()
    load_slab.wait()
    for group in range(4):
        for which, by in enumerate((3, 2, 1)):
            source = lax.rem(grp + by, 4)

            @pl.when(source < GROUPS[group][2])
            def _():
                slab_copy(which, group, source, up).wait_recv()
    load_rows.wait()

    def split_factor(c, _):
        at = pl.ds(pl.multiple_of(c * R, R), R)
        row = lax.broadcasted_iota(jnp.int32, (R, B), 0) + c * R
        col = lax.broadcasted_iota(jnp.int32, (R, B), 1)
        hi, lo = split(jnp.where(row <= col, factor[at, :], 0.0))
        fac_hi[at, :] = hi
        fac_lo[at, :] = lo
        return 0

    lax.fori_loop(0, C, split_factor, 0)
    alive = (grp < live[0]).astype(jnp.float32)

    def near_copy(side, c):
        at = pl.ds(pl.multiple_of(c * R, R), R)
        return pltpu.make_async_remote_copy(
            solved.at[at], gath.at[2 if side == 0 else 0, at],
            near_send.at[side, c], near_recv.at[side, c],
            device_id=up if side == 0 else down, device_id_type=MESH,
        )

    def fwd_copy(side, c):
        at = pl.ds(pl.multiple_of(c * R + side * (R // 2), R // 2), R // 2)
        return pltpu.make_async_remote_copy(
            gath.at[2 if side == 0 else 0, at], gath.at[1, at],
            fwd_send.at[side, c], fwd_recv.at[side, c],
            device_id=up if side == 0 else down, device_id_type=MESH,
        )

    def put_halves(slot, c, x):
        hi, lo = split(x)
        halves[slot, pl.ds(pl.multiple_of(c * 2 * R, 2 * R), R), :] = hi
        halves[slot, pl.ds(pl.multiple_of(c * 2 * R + R, R), R), :] = lo

    def solve_send(c):
        at = pl.ds(pl.multiple_of(c * R, R), R)
        hi, lo = split(rows[at, :])
        both = jnp.concatenate([hi, lo], axis=0)
        for j in range(3):
            k = 256 * (j + 1)
            cols = pl.ds(256 * j, 256)
            x = jnp.dot(both[:, :k], fac_hi[pl.ds(0, k), cols], preferred_element_type=jnp.float32)
            y = jnp.dot(hi[:, :k], fac_lo[pl.ds(0, k), cols], preferred_element_type=jnp.float32)
            solved[at, cols] = alive * (x[:R] + (x[R:] + y))
        near_copy(0, c).start()
        near_copy(1, c).start()
        put_halves(0, c, solved[at, :])

    def near_wait_forward(c):
        near_copy(0, c).wait_recv()
        fwd_copy(0, c).start()
        near_copy(1, c).wait_recv()
        fwd_copy(1, c).start()

    def first_two(c, _):
        solve_send(c)
        return 0

    lax.fori_loop(0, 2, first_two, 0)
    near_wait_forward(0)

    lefts = [lax.rem(first[0, 0, p] - grp + 4, 4) for p in range(PAIRS)]
    rights = [lax.rem(second[0, 0, p] - grp + 4, 4) for p in range(PAIRS)]
    dists = (3 - 2 * core, 1 + 2 * core, 2, 4, 0)
    weights = [
        [(offset[0, 0, p] == d).astype(jnp.float32) for p in range(PAIRS)] for d in dists
    ]

    def part_copy(n):
        return pltpu.make_async_remote_copy(
            out.at[n, pl.ds(0, 2)], part.at[n], part_send.at[n], part_recv.at[n],
            device_id=partner, device_id_type=MESH,
        )

    def one_copy(n):
        return pltpu.make_async_remote_copy(
            out.at[n, 2], xin.at[n, 0], one_send.at[n], one_recv.at[n],
            device_id=dev(2, 0), device_id_type=MESH,
        )

    def two_copy(n):
        return pltpu.make_async_remote_copy(
            out.at[n, 3], xin.at[n, 1], two_send.at[n], two_recv.at[n],
            device_id=dev(4, 0), device_id_type=MESH,
        )

    def combine_send(n):
        part_copy(n).wait_recv()
        out[n, 2] = out[n, 2] + part[n, 0]
        one_copy(n).start()
        out[n, 3 + core] = out[n, 3 + core] + part[n, 1]
        two_copy(n).start()

    def tile(c, k):
        n = c * c + k
        is_row = k <= c
        i = jnp.where(is_row, c, k - c - 1)
        j = jnp.where(is_row, k, c)
        at_i = pl.ds(pl.multiple_of(i * 2 * R, 2 * R), 2 * R)
        at_j = pl.ds(pl.multiple_of(j * 2 * R, 2 * R), 2 * R)
        for p in range(PAIRS):
            x = lax.dot_general(
                halves[lefts[p], at_i, :], halves[rights[p], at_j, :], NT,
                preferred_element_type=jnp.float32,
            )
            terms[p] = (x[:R, :R] + (x[R:, :R] + x[:R, R:])) + x[R:, R:]
        def mix(r, _):
            at = pl.ds(pl.multiple_of(r * 16, 16), 16)
            t = [terms[p, at, :] for p in range(PAIRS)]
            for slot in range(5):
                w = weights[slot]
                total = w[0] * t[0]
                for p in range(1, PAIRS):
                    total = total + w[p] * t[p]
                out[n, slot, at, :] = total
            return 0

        lax.fori_loop(0, R // 16, mix, 0, unroll=True)
        part_copy(n).start()

        @pl.when(k > 0)
        def _():
            combine_send(n - 1)

    def step(c, _):
        @pl.when(c + 2 < C)
        def _():
            solve_send(c + 2)

        @pl.when(c + 1 < C)
        def _():
            near_wait_forward(c + 1)

        at = pl.ds(pl.multiple_of(c * R, R), R)
        put_halves(1, c, gath[0, at, :])
        put_halves(3, c, gath[2, at, :])
        fwd_copy(0, c).wait_recv()
        fwd_copy(1, c).wait_recv()
        put_halves(2, c, gath[1, at, :])

        def one_tile(k, _):
            tile(c, k)
            return 0

        lax.fori_loop(0, 2 * c + 1, one_tile, 0)
        combine_send(c * c + 2 * c)
        return 0

    lax.fori_loop(0, C, step, 0)
    store_solved = pltpu.make_async_copy(solved, solved_out.at[0, 0], local_sem.at[0])
    store_solved.start()
    load_base.wait()

    def finish(c, _):
        def one(k, _):
            n = c * c + k
            is_row = k <= c
            i = jnp.where(is_row, c, k - c - 1)
            j = jnp.where(is_row, k, c)
            at_i = pl.ds(pl.multiple_of(i * R, R), R)
            at_j = pl.ds(pl.multiple_of(j * R, R), R)
            one_copy(n).wait_recv()
            two_copy(n).wait_recv()
            upd[at_i, at_j] = base[at_i, at_j] - (out[n, 4] + (xin[n, 0] + xin[n, 1]))
            return 0

        lax.fori_loop(0, 2 * c + 1, one, 0)
        return 0

    lax.fori_loop(0, C, finish, 0)
    store_updated = pltpu.make_async_copy(upd, updated_out.at[0, 0], local_sem.at[1])
    store_updated.start()

    for group in range(4):
        @pl.when(grp < GROUPS[group][2])
        def _():
            for which, target in enumerate((up, across, down)):
                slab_copy(which, group, grp, target).wait_send()

    def drain_chunk(c, _):
        for side in range(2):
            near_copy(side, c).wait_send()
            fwd_copy(side, c).wait_send()
        return 0

    def drain_tile(n, _):
        part_copy(n).wait_send()
        one_copy(n).wait_send()
        two_copy(n).wait_send()
        return 0

    lax.fori_loop(0, C, drain_chunk, 0)
    lax.fori_loop(0, TILES, drain_tile, 0)
    store_solved.wait()
    store_updated.wait()


def shards(panel, diag_inverse, ancestor, live_blocks, pair_first, pair_second, pair_offset):
    f32, bf16 = jnp.float32, jnp.bfloat16
    dma = pltpu.SemaphoreType.DMA
    smem = pl.BlockSpec(memory_space=pltpu.SMEM)
    raw = pl.BlockSpec(memory_space=pl.ANY)
    block = jax.ShapeDtypeStruct((1, 1, B, B), f32)
    return pl.pallas_call(
        kernel,
        out_shape=(block, block),
        in_specs=[smem] * 4 + [raw] * 3,
        out_specs=(raw, raw),
        scratch_shapes=[
            pltpu.VMEM((B, B), f32),
            pltpu.VMEM((B, B), bf16),
            pltpu.VMEM((B, B), bf16),
            pltpu.VMEM((B, B), f32),
            pltpu.VMEM((B, B), f32),
            pltpu.VMEM((3, B, B), f32),
            pltpu.VMEM((4, 2 * B, B), bf16),
            pltpu.VMEM((TILES, 5, R, R), f32),
            pltpu.VMEM((TILES, 2, R, R), f32),
            pltpu.VMEM((TILES, 2, R, R), f32),
            pltpu.VMEM((B, B), f32),
            pltpu.VMEM((B, B), f32),
            pltpu.VMEM((PAIRS, R, R), f32),
            dma((3,)),
            dma((3, 4)),
            dma((3, 4)),
            dma((2, C)),
            dma((2, C)),
            dma((2, C)),
            dma((2, C)),
            dma((TILES,)),
            dma((TILES,)),
            dma((TILES,)),
            dma((TILES,)),
            dma((TILES,)),
            dma((TILES,)),
        ],
        compiler_params=pltpu.CompilerParams(
            collective_id=0, has_side_effects=True, vmem_limit_bytes=60 * 2**20
        ),
    )(live_blocks, pair_first, pair_second, pair_offset, panel, diag_inverse, ancestor)


def solution(mesh):
    placed = (
        P("own", "grp", None, None),
        P("own", "grp", None),
        P("own", "grp", None, None),
        P("own"),
        P("own", "grp", None),
        P("own", "grp", None),
        P("own", "grp", None),
    )
    return jax.shard_map(
        shards,
        mesh=mesh,
        in_specs=placed,
        out_specs=(P("own", "grp", None, None), P("own", "grp", None, None)),
        check_vma=False,
    )
```

time: 481 us -> 202 us (0.42)
  the two profiles are of different devices: /device:TPU:1 before, /device:TPU:202 now
where the time goes in v1:
time: 202 us
  Pallas kernels  196 us (97%)
  local copies, waits for them, and re-layouts  4.78 us (2%)
    pallas_call x1, Pallas kernels, shards(): pl.pallas_call(kernel, out_shape=(block, block), in_specs=[smem] * 4 + [r...  196 us
    unnamed x4, local copies, waits for them, and re-layouts  4.78 us

profile of v1, /device:TPU:202, one launch (start us, length us, event | category | flops | bytes accessed | tf_op | source)
XLA Modules:
  0.0 201.9 jit_solution(7761290342400545759)
XLA Ops:
  1.3 195.8 %shard_map.86 = (f32[1,1,768,768]{3,2,1,0:T(8,128)}, f32[1,1,768,768]{3,2,1,0:T(8,128)}) custom-call(s32[1]{0:T(128)S(6)} %copy.11.live, s32[1,1,7]{2,1,0:T(1,128)} %first.1, s32[1,1,7]{2,1,0:T(1,128)} %second.1, s32[1,1,7]{2,1,0:T(1,128)} %offset.1, f32[1,1,768,768]{3,2,1,0:T(8,128)} %panel.1, f32[1,192,768]{2,1,0:T(8,128)} %diag.1, f32[1,1,768,768]{3,2,1,0:T(8,128)} %anc.1), custom_call_target="tpu_custom_call" | custom-call | tf_op jit(solution)/shard_map/pallas_call | solution.py:283
  197.1 0.0 copy-start
  197.1 3.4 %copy.12 = f32[1,1,768,768]{3,2,1,0:T(8,128)} copy(f32[1,1,768,768]{3,2,1,0:T(8,128)} %get-tuple-element.4) | data formatting | bytes 4718592
  200.5 0.0 copy-done
  200.5 1.4 copy.13
Async XLA Ops:
  197.1 3.4 %copy-start = (f32[1,1,768,768]{3,2,1,0:T(8,128)S(1)}, f32[1,1,768,768]{3,2,1,0:T(8,128)}, u32[]{:S(2)}) copy-start(f32[1,1,768,768]{3,2,1,0:T(8,128)} %get-tuple-element.5) | copy-start | bytes 7077892

commit v2 on v1

--- a/solution.py
+++ b/solution.py
@@ -10,7 +10,9 @@
 PAIRS = 7
 R = 128
 C = B // R
+H = R // 2
 TILES = C * C
+MID = 4
 SLAB = B // 4
 GROUPS = ((0, 128, 1), (128, 256, 2), (384, 128, 3), (512, 256, 4))
 NT = (((1,), (1,)), ((), ()))
@@ -25,9 +27,9 @@
 def kernel(
     live, first, second, offset, panel, diag, anc,
     solved_out, updated_out,
-    factor, fac_hi, fac_lo, rows, solved, gath, halves, out, part, xin, base, upd, terms,
-    local_sem, fac_send, fac_recv, near_send, near_recv, fwd_send, fwd_recv,
-    part_send, part_recv, one_send, one_recv, two_send, two_recv,
+    factor, fac_hi, fac_lo, rows, solved, mine, gath, halves, out, part, xin, base, upd, terms,
+    packed, pairs_in, pairs, local_sem, pairs_sem, fac_send, fac_recv, shift_send, shift_recv,
+    near_send, near_recv, fwd_send, fwd_recv, part_send, part_recv, low_send, low_recv, high_send, high_recv,
 ):
     own = lax.axis_index("own")
     grp = lax.axis_index("grp")
@@ -44,7 +46,8 @@
     load_rows.start()
     load_base.start()
     barrier = pltpu.get_barrier_semaphore()
-    peers = (up, down, across, partner, dev(2, 0), dev(-2, 0), dev(4, 0), dev(-4, 0))
+    after, before = dev(2, 0), dev(-2, 0)
+    peers = (up, down, across, partner, after, before)
     for peer in peers:
         pl.semaphore_signal(barrier, 1, device_id=peer, device_id_type=MESH)
     pl.semaphore_wait(barrier, len(peers))
@@ -63,6 +66,17 @@
         def _():
             for which, target in enumerate((up, across, down)):
                 slab_copy(which, group, grp, target).start()
+
+    spot = lax.broadcasted_iota(jnp.int32, (8, 128), 1) + 128 * lax.broadcasted_iota(jnp.int32, (8, 128), 0)
+    values = jnp.zeros((8, 128), jnp.int32)
+    for row, source in enumerate((first, second, offset)):
+        for p in range(PAIRS):
+            values = jnp.where(spot == 128 * row + p, source[0, 0, p], values)
+    packed[...] = values
+    pairs_copy = pltpu.make_async_remote_copy(
+        packed, pairs_in, pairs_sem.at[0], pairs_sem.at[1], device_id=after, device_id_type=MESH
+    )
+    pairs_copy.start()
 
     load_slab = pltpu.make_async_copy(
         diag.at[0], factor.at[pl.ds(pl.multiple_of(grp * SLAB, SLAB), SLAB)], local_sem.at[2]
@@ -90,16 +104,23 @@
     lax.fori_loop(0, C, split_factor, 0)
     alive = (grp < live[0]).astype(jnp.float32)
 
-    def near_copy(side, c):
-        at = pl.ds(pl.multiple_of(c * R, R), R)
-        return pltpu.make_async_remote_copy(
-            solved.at[at], gath.at[2 if side == 0 else 0, at],
-            near_send.at[side, c], near_recv.at[side, c],
+    def shift_copy(m):
+        at = pl.ds(pl.multiple_of(m * H, H), H)
+        return pltpu.make_async_remote_copy(
+            solved.at[at], mine.at[at], shift_send.at[m], shift_recv.at[m],
+            device_id=after, device_id_type=MESH,
+        )
+
+    def near_copy(side, m):
+        at = pl.ds(pl.multiple_of(m * H, H), H)
+        return pltpu.make_async_remote_copy(
+            mine.at[at], gath.at[2 if side == 0 else 0, at],
+            near_send.at[side, m], near_recv.at[side, m],
             device_id=up if side == 0 else down, device_id_type=MESH,
         )
 
     def fwd_copy(side, c):
-        at = pl.ds(pl.multiple_of(c * R + side * (R // 2), R // 2), R // 2)
+        at = pl.ds(pl.multiple_of(c * R + side * H, H), H)
         return pltpu.make_async_remote_copy(
             gath.at[2 if side == 0 else 0, at], gath.at[1, at],
             fwd_send.at[side, c], fwd_recv.at[side, c],
@@ -111,7 +132,7 @@
         halves[slot, pl.ds(pl.multiple_of(c * 2 * R, 2 * R), R), :] = hi
         halves[slot, pl.ds(pl.multiple_of(c * 2 * R + R, R), R), :] = lo
 
-    def solve_send(c):
+    def solve_shift(c, _):
         at = pl.ds(pl.multiple_of(c * R, R), R)
         hi, lo = split(rows[at, :])
         both = jnp.concatenate([hi, lo], axis=0)
@@ -121,28 +142,41 @@
             x = jnp.dot(both[:, :k], fac_hi[pl.ds(0, k), cols], preferred_element_type=jnp.float32)
             y = jnp.dot(hi[:, :k], fac_lo[pl.ds(0, k), cols], preferred_element_type=jnp.float32)
             solved[at, cols] = alive * (x[:R] + (x[R:] + y))
-        near_copy(0, c).start()
-        near_copy(1, c).start()
-        put_halves(0, c, solved[at, :])
-
-    def near_wait_forward(c):
-        near_copy(0, c).wait_recv()
+        shift_copy(2 * c).start()
+        shift_copy(2 * c + 1).start()
+        return 0
+
+    def near_start(c):
+        shift_copy(2 * c).wait_recv()
+        near_copy(0, 2 * c).start()
+        shift_copy(2 * c + 1).wait_recv()
+        near_copy(1, 2 * c + 1).start()
+        near_copy(0, 2 * c + 1).start()
+        near_copy(1, 2 * c).start()
+        put_halves(0, c, mine[pl.ds(pl.multiple_of(c * R, R), R), :])
+
+    def forward(c):
+        near_copy(0, 2 * c).wait_recv()
         fwd_copy(0, c).start()
-        near_copy(1, c).wait_recv()
+        near_copy(1, 2 * c + 1).wait_recv()
         fwd_copy(1, c).start()
 
-    def first_two(c, _):
-        solve_send(c)
-        return 0
-
-    lax.fori_loop(0, 2, first_two, 0)
-    near_wait_forward(0)
-
-    lefts = [lax.rem(first[0, 0, p] - grp + 4, 4) for p in range(PAIRS)]
-    rights = [lax.rem(second[0, 0, p] - grp + 4, 4) for p in range(PAIRS)]
-    dists = (3 - 2 * core, 1 + 2 * core, 2, 4, 0)
+    lax.fori_loop(0, C, solve_shift, 0)
+    store_solved = pltpu.make_async_copy(solved, solved_out.at[0, 0], local_sem.at[0])
+    store_solved.start()
+    near_start(0)
+    pairs_copy.wait_recv()
+    load_pairs = pltpu.make_async_copy(pairs_in, pairs, local_sem.at[2])
+    load_pairs.start()
+    load_pairs.wait()
+    forward(0)
+    near_start(1)
+
+    lefts = [lax.rem(pairs[0, p] - grp + 4, 4) for p in range(PAIRS)]
+    rights = [lax.rem(pairs[1, p] - grp + 4, 4) for p in range(PAIRS)]
+    dists = (1 + 2 * core, 3 - 2 * core, 0, 4, 2)
     weights = [
-        [(offset[0, 0, p] == d).astype(jnp.float32) for p in range(PAIRS)] for d in dists
+        [(pairs[2, p] == d).astype(jnp.float32) for p in range(PAIRS)] for d in dists
     ]
 
     def part_copy(n):
@@ -151,24 +185,24 @@
             device_id=partner, device_id_type=MESH,
         )
 
-    def one_copy(n):
-        return pltpu.make_async_remote_copy(
-            out.at[n, 2], xin.at[n, 0], one_send.at[n], one_recv.at[n],
-            device_id=dev(2, 0), device_id_type=MESH,
-        )
-
-    def two_copy(n):
-        return pltpu.make_async_remote_copy(
-            out.at[n, 3], xin.at[n, 1], two_send.at[n], two_recv.at[n],
-            device_id=dev(4, 0), device_id_type=MESH,
+    def low_copy(n):
+        return pltpu.make_async_remote_copy(
+            out.at[n, 2], xin.at[n, 0], low_send.at[n], low_recv.at[n],
+            device_id=before, device_id_type=MESH,
+        )
+
+    def high_copy(n):
+        return pltpu.make_async_remote_copy(
+            out.at[n, 3], xin.at[n, 1], high_send.at[n], high_recv.at[n],
+            device_id=after, device_id_type=MESH,
         )
 
     def combine_send(n):
         part_copy(n).wait_recv()
-        out[n, 2] = out[n, 2] + part[n, 0]
-        one_copy(n).start()
-        out[n, 3 + core] = out[n, 3 + core] + part[n, 1]
-        two_copy(n).start()
+        out[n, 3 - core] = out[n, 3 - core] + part[n, 0]
+        low_copy(n).start()
+        high_copy(n).start()
+        out[n, 4] = out[n, 4] + part[n, 1]
 
     def tile(c, k):
         n = c * c + k
@@ -201,36 +235,7 @@
         def _():
             combine_send(n - 1)
 
-    def step(c, _):
-        @pl.when(c + 2 < C)
-        def _():
-            solve_send(c + 2)
-
-        @pl.when(c + 1 < C)
-        def _():
-            near_wait_forward(c + 1)
-
-        at = pl.ds(pl.multiple_of(c * R, R), R)
-        put_halves(1, c, gath[0, at, :])
-        put_halves(3, c, gath[2, at, :])
-        fwd_copy(0, c).wait_recv()
-        fwd_copy(1, c).wait_recv()
-        put_halves(2, c, gath[1, at, :])
-
-        def one_tile(k, _):
-            tile(c, k)
-            return 0
-
-        lax.fori_loop(0, 2 * c + 1, one_tile, 0)
-        combine_send(c * c + 2 * c)
-        return 0
-
-    lax.fori_loop(0, C, step, 0)
-    store_solved = pltpu.make_async_copy(solved, solved_out.at[0, 0], local_sem.at[0])
-    store_solved.start()
-    load_base.wait()
-
-    def finish(c, _):
+    def finish(c):
         def one(k, _):
             n = c * c + k
             is_row = k <= c
@@ -238,17 +243,59 @@
             j = jnp.where(is_row, k, c)
             at_i = pl.ds(pl.multiple_of(i * R, R), R)
             at_j = pl.ds(pl.multiple_of(j * R, R), R)
-            one_copy(n).wait_recv()
-            two_copy(n).wait_recv()
+            low_copy(n).wait_recv()
+            high_copy(n).wait_recv()
             upd[at_i, at_j] = base[at_i, at_j] - (out[n, 4] + (xin[n, 0] + xin[n, 1]))
             return 0
 
         lax.fori_loop(0, 2 * c + 1, one, 0)
-        return 0
-
-    lax.fori_loop(0, C, finish, 0)
-    store_updated = pltpu.make_async_copy(upd, updated_out.at[0, 0], local_sem.at[1])
-    store_updated.start()
+
+    load_base.wait()
+
+    def step(c, _):
+        @pl.when(c >= 2)
+        def _():
+            finish(c - 2)
+
+        at = pl.ds(pl.multiple_of(c * R, R), R)
+        near_copy(0, 2 * c + 1).wait_recv()
+        near_copy(1, 2 * c).wait_recv()
+        put_halves(1, c, gath[0, at, :])
+        put_halves(3, c, gath[2, at, :])
+        fwd_copy(0, c).wait_recv()
+        fwd_copy(1, c).wait_recv()
+        put_halves(2, c, gath[1, at, :])
+
+        def one_tile(k, _):
+            tile(c, k)
+
+            @pl.when(jnp.logical_and(k == jnp.minimum(MID, 2 * c), c + 1 < C))
+            def _():
+                forward(c + 1)
+
+                @pl.when(c + 2 < C)
+                def _():
+                    near_start(c + 2)
+
+            return 0
+
+        lax.fori_loop(0, 2 * c + 1, one_tile, 0)
+        combine_send(c * c + 2 * c)
+        return 0
+
+    lax.fori_loop(0, C, step, 0)
+    finish(C - 2)
+    edge = B - R
+    stores = [
+        pltpu.make_async_copy(upd.at[pl.ds(r, h), pl.ds(c, w)], updated_out.at[0, 0, pl.ds(r, h), pl.ds(c, w)], sem)
+        for r, h, c, w, sem in (
+            (0, edge, 0, edge, local_sem.at[1]), (edge, R, 0, B, local_sem.at[2]), (0, edge, edge, R, local_sem.at[3])
+        )
+    ]
+    stores[0].start()
+    finish(C - 1)
+    stores[1].start()
+    stores[2].start()
 
     for group in range(4):
         @pl.when(grp < GROUPS[group][2])
@@ -256,22 +303,31 @@
             for which, target in enumerate((up, across, down)):
                 slab_copy(which, group, grp, target).wait_send()
 
+    pairs_copy.wait_send()
+
+    def drain_piece(m, _):
+        shift_copy(m).wait_send()
+        for side in range(2):
+            near_copy(side, m).wait_send()
+        return 0
+
     def drain_chunk(c, _):
         for side in range(2):
-            near_copy(side, c).wait_send()
             fwd_copy(side, c).wait_send()
         return 0
 
     def drain_tile(n, _):
         part_copy(n).wait_send()
-        one_copy(n).wait_send()
-        two_copy(n).wait_send()
-        return 0
-
+        low_copy(n).wait_send()
+        high_copy(n).wait_send()
+        return 0
+
+    lax.fori_loop(0, 2 * C, drain_piece, 0)
     lax.fori_loop(0, C, drain_chunk, 0)
     lax.fori_loop(0, TILES, drain_tile, 0)
     store_solved.wait()
-    store_updated.wait()
+    for store in stores:
+        store.wait()
 
 
 def shards(panel, diag_inverse, ancestor, live_blocks, pair_first, pair_second, pair_offset):
@@ -291,6 +347,7 @@
             pltpu.VMEM((B, B), bf16),
             pltpu.VMEM((B, B), f32),
             pltpu.VMEM((B, B), f32),
+            pltpu.VMEM((B, B), f32),
             pltpu.VMEM((3, B, B), f32),
             pltpu.VMEM((4, 2 * B, B), bf16),
             pltpu.VMEM((TILES, 5, R, R), f32),
@@ -299,11 +356,17 @@
             pltpu.VMEM((B, B), f32),
             pltpu.VMEM((B, B), f32),
             pltpu.VMEM((PAIRS, R, R), f32),
-            dma((3,)),
+            pltpu.VMEM((8, 128), jnp.int32),
+            pltpu.VMEM((8, 128), jnp.int32),
+            pltpu.SMEM((8, 128), jnp.int32),
+            dma((4,)),
+            dma((2,)),
             dma((3, 4)),
             dma((3, 4)),
-            dma((2, C)),
-            dma((2, C)),
+            dma((2 * C,)),
+            dma((2 * C,)),
+            dma((2, 2 * C)),
+            dma((2, 2 * C)),
             dma((2, C)),
             dma((2, C)),
             dma((TILES,)),

time: 202 us -> 162 us (0.80)
  the two profiles are of different devices: /device:TPU:202 before, /device:TPU:1 now
where the time goes in v2:
time: 162 us
  Pallas kernels  155 us (96%)
  local copies, waits for them, and re-layouts  4.78 us (3%)
    pallas_call x1, Pallas kernels, shards(): pl.pallas_call(kernel, out_shape=(block, block), in_specs=[smem] * 4 + [r...  155 us
    unnamed x4, local copies, waits for them, and re-layouts  4.78 us

profile of v2, /device:TPU:1, one launch (start us, length us, event | category | flops | bytes accessed | tf_op | source)
XLA Modules:
  0.0 161.5 jit_solution(983987407711040271)
XLA Ops:
  1.3 155.4 %shard_map.86 = (f32[1,1,768,768]{3,2,1,0:T(8,128)}, f32[1,1,768,768]{3,2,1,0:T(8,128)}) custom-call(s32[1]{0:T(128)S(6)} %copy.11.live, s32[1,1,7]{2,1,0:T(1,128)} %first.1, s32[1,1,7]{2,1,0:T(1,128)} %second.1, s32[1,1,7]{2,1,0:T(1,128)} %offset.1, f32[1,1,768,768]{3,2,1,0:T(8,128)} %panel.1, f32[1,192,768]{2,1,0:T(8,128)} %diag.1, f32[1,1,768,768]{3,2,1,0:T(8,128)} %anc.1), custom_call_target="tpu_custom_call" | custom-call | tf_op jit(solution)/shard_map/pallas_call | solution.py:339
  156.7 0.0 copy-start
  156.7 3.4 %copy.12 = f32[1,1,768,768]{3,2,1,0:T(8,128)} copy(f32[1,1,768,768]{3,2,1,0:T(8,128)} %get-tuple-element.4) | data formatting | bytes 4718592
  160.1 0.0 copy-done
  160.1 1.4 copy.13
Async XLA Ops:
  156.7 3.4 %copy-start = (f32[1,1,768,768]{3,2,1,0:T(8,128)S(1)}, f32[1,1,768,768]{3,2,1,0:T(8,128)}, u32[]{:S(2)}) copy-start(f32[1,1,768,768]{3,2,1,0:T(8,128)} %get-tuple-element.5) | copy-start | bytes 7077892

commit v3 on v2

--- a/solution.py
+++ b/solution.py
@@ -13,6 +13,8 @@
 H = R // 2
 TILES = C * C
 MID = 4
+AHEAD = 2
+LAG = 2
 SLAB = B // 4
 GROUPS = ((0, 128, 1), (128, 256, 2), (384, 128, 3), (512, 256, 4))
 NT = (((1,), (1,)), ((), ()))
@@ -39,7 +41,7 @@
         return (lax.rem(own + by_own + 64, 64), lax.rem(grp + by_grp + 4, 4))
 
     partner = (own + 1 - 2 * core, grp)
-    up, down, across = dev(0, 1), dev(0, -1), dev(0, 2)
+    up, down = dev(0, 1), dev(0, -1)
 
     load_rows = pltpu.make_async_copy(panel.at[0, 0], rows, local_sem.at[0])
     load_base = pltpu.make_async_copy(anc.at[0, 0], base, local_sem.at[1])
@@ -47,11 +49,20 @@
     load_base.start()
     barrier = pltpu.get_barrier_semaphore()
     after, before = dev(2, 0), dev(-2, 0)
-    peers = (up, down, across, partner, after, before)
+    peers = (up, down, partner, after, before)
     for peer in peers:
         pl.semaphore_signal(barrier, 1, device_id=peer, device_id_type=MESH)
     pl.semaphore_wait(barrier, len(peers))
 
+    def slab_fwd(side, group, slab):
+        start, width, _ = GROUPS[group]
+        at = pl.multiple_of(slab * SLAB + side * (SLAB // 2), SLAB // 2)
+        place = factor.at[pl.ds(at, SLAB // 2), pl.ds(start, width)]
+        return pltpu.make_async_remote_copy(
+            place, place, fac_send.at[2 + side, group], fac_recv.at[2 + side, group],
+            device_id=up if side == 0 else down, device_id_type=MESH,
+        )
+
     def slab_copy(which, group, source_slab, target):
         start, width, _ = GROUPS[group]
         place = factor.at[pl.ds(pl.multiple_of(source_slab * SLAB, SLAB), SLAB), pl.ds(start, width)]
@@ -61,10 +72,10 @@
             device_id=target, device_id_type=MESH,
         )
 
-    for group in range(4):
+    for group in (3, 1, 2, 0):
         @pl.when(grp < GROUPS[group][2])
         def _():
-            for which, target in enumerate((up, across, down)):
+            for which, target in enumerate((up, down)):
                 slab_copy(which, group, grp, target).start()
 
     spot = lax.broadcasted_iota(jnp.int32, (8, 128), 1) + 128 * lax.broadcasted_iota(jnp.int32, (8, 128), 0)
@@ -82,14 +93,20 @@
         diag.at[0], factor.at[pl.ds(pl.multiple_of(grp * SLAB, SLAB), SLAB)], local_sem.at[2]
     )
     load_slab.start()
+    below, above, opposite = (lax.rem(grp + by, 4) for by in (3, 1, 2))
+    for group in (3, 1, 2, 0):
+        for side, slab in enumerate((below, above)):
+            @pl.when(slab < GROUPS[group][2])
+            def _():
+                slab_copy(side, group, slab, up).wait_recv()
+                slab_fwd(side, group, slab).start()
+
     load_slab.wait()
-    for group in range(4):
-        for which, by in enumerate((3, 2, 1)):
-            source = lax.rem(grp + by, 4)
-
-            @pl.when(source < GROUPS[group][2])
-            def _():
-                slab_copy(which, group, source, up).wait_recv()
+    for group in (3, 1, 2, 0):
+        @pl.when(opposite < GROUPS[group][2])
+        def _():
+            for side in range(2):
+                slab_fwd(side, group, opposite).wait_recv()
     load_rows.wait()
 
     def split_factor(c, _):
@@ -142,11 +159,22 @@
             x = jnp.dot(both[:, :k], fac_hi[pl.ds(0, k), cols], preferred_element_type=jnp.float32)
             y = jnp.dot(hi[:, :k], fac_lo[pl.ds(0, k), cols], preferred_element_type=jnp.float32)
             solved[at, cols] = alive * (x[:R] + (x[R:] + y))
+
+        @pl.when(c < AHEAD)
+        def _():
+            shift_start(c)
+
+        return 0
+
+    def shift_start(c):
         shift_copy(2 * c).start()
         shift_copy(2 * c + 1).start()
-        return 0
 
     def near_start(c):
+        @pl.when(c + AHEAD < C)
+        def _():
+            shift_start(c + AHEAD)
+
         shift_copy(2 * c).wait_recv()
         near_copy(0, 2 * c).start()
         shift_copy(2 * c + 1).wait_recv()
@@ -164,13 +192,13 @@
     lax.fori_loop(0, C, solve_shift, 0)
     store_solved = pltpu.make_async_copy(solved, solved_out.at[0, 0], local_sem.at[0])
     store_solved.start()
-    near_start(0)
+    near_start(jnp.int32(0))
     pairs_copy.wait_recv()
     load_pairs = pltpu.make_async_copy(pairs_in, pairs, local_sem.at[2])
     load_pairs.start()
     load_pairs.wait()
     forward(0)
-    near_start(1)
+    near_start(jnp.int32(1))
 
     lefts = [lax.rem(pairs[0, p] - grp + 4, 4) for p in range(PAIRS)]
     rights = [lax.rem(pairs[1, p] - grp + 4, 4) for p in range(PAIRS)]
@@ -231,9 +259,9 @@
         lax.fori_loop(0, R // 16, mix, 0, unroll=True)
         part_copy(n).start()
 
-        @pl.when(k > 0)
-        def _():
-            combine_send(n - 1)
+        @pl.when(k >= LAG)
+        def _():
+            combine_send(n - LAG)
 
     def finish(c):
         def one(k, _):
@@ -280,7 +308,12 @@
             return 0
 
         lax.fori_loop(0, 2 * c + 1, one_tile, 0)
-        combine_send(c * c + 2 * c)
+
+        def rest(k, _):
+            combine_send(c * c + k)
+            return 0
+
+        lax.fori_loop(jnp.maximum(2 * c + 1 - LAG, 0), 2 * c + 1, rest, 0)
         return 0
 
     lax.fori_loop(0, C, step, 0)
@@ -300,8 +333,13 @@
     for group in range(4):
         @pl.when(grp < GROUPS[group][2])
         def _():
-            for which, target in enumerate((up, across, down)):
+            for which, target in enumerate((up, down)):
                 slab_copy(which, group, grp, target).wait_send()
+
+        for side, slab in enumerate((below, above)):
+            @pl.when(slab < GROUPS[group][2])
+            def _():
+                slab_fwd(side, group, slab).wait_send()
 
     pairs_copy.wait_send()
 
@@ -361,8 +399,8 @@
             pltpu.SMEM((8, 128), jnp.int32),
             dma((4,)),
             dma((2,)),
-            dma((3, 4)),
-            dma((3, 4)),
+            dma((4, 4)),
+            dma((4, 4)),
             dma((2 * C,)),
             dma((2 * C,)),
             dma((2, 2 * C)),

time: 162 us -> 150 us (0.926)
  Pallas kernels: 155 us -> 144 us
    pallas_call x1, Pallas kernels: 155 us -> 144 us  [shards(): pl.pallas_call(kernel, out_shape=(block, block), in_specs=[smem] * 4 + [r...]
where the time goes in v3:
time: 150 us
  Pallas kernels  144 us (96%)
  local copies, waits for them, and re-layouts  4.78 us (3%)
    pallas_call x1, Pallas kernels, shards(): pl.pallas_call(kernel, out_shape=(block, block), in_specs=[smem] * 4 + [r...  144 us
    unnamed x4, local copies, waits for them, and re-layouts  4.78 us

profile of v3, /device:TPU:1, one launch (start us, length us, event | category | flops | bytes accessed | tf_op | source)
XLA Modules:
  0.0 150.2 jit_solution(16082323529570825745)
XLA Ops:
  1.3 144.1 %shard_map.86 = (f32[1,1,768,768]{3,2,1,0:T(8,128)}, f32[1,1,768,768]{3,2,1,0:T(8,128)}) custom-call(s32[1]{0:T(128)S(6)} %copy.11.live, s32[1,1,7]{2,1,0:T(1,128)} %first.1, s32[1,1,7]{2,1,0:T(1,128)} %second.1, s32[1,1,7]{2,1,0:T(1,128)} %offset.1, f32[1,1,768,768]{3,2,1,0:T(8,128)} %panel.1, f32[1,192,768]{2,1,0:T(8,128)} %diag.1, f32[1,1,768,768]{3,2,1,0:T(8,128)} %anc.1), custom_call_target="tpu_custom_call" | custom-call | tf_op jit(solution)/shard_map/pallas_call | solution.py:377
  145.4 0.0 copy-start
  145.4 3.4 %copy.12 = f32[1,1,768,768]{3,2,1,0:T(8,128)} copy(f32[1,1,768,768]{3,2,1,0:T(8,128)} %get-tuple-element.4) | data formatting | bytes 4718592
  148.8 0.0 copy-done
  148.8 1.4 copy.13
Async XLA Ops:
  145.4 3.4 %copy-start = (f32[1,1,768,768]{3,2,1,0:T(8,128)S(1)}, f32[1,1,768,768]{3,2,1,0:T(8,128)}, u32[]{:S(2)}) copy-start(f32[1,1,768,768]{3,2,1,0:T(8,128)} %get-tuple-element.5) | copy-start | bytes 7077892

commit v4 on v3

--- a/solution.py
+++ b/solution.py
@@ -11,6 +11,7 @@
 R = 128
 C = B // R
 H = R // 2
+Q = R // 4
 TILES = C * C
 MID = 4
 AHEAD = 2
@@ -122,14 +123,14 @@
     alive = (grp < live[0]).astype(jnp.float32)
 
     def shift_copy(m):
-        at = pl.ds(pl.multiple_of(m * H, H), H)
+        at = pl.ds(pl.multiple_of(m * Q, Q), Q)
         return pltpu.make_async_remote_copy(
             solved.at[at], mine.at[at], shift_send.at[m], shift_recv.at[m],
             device_id=after, device_id_type=MESH,
         )
 
     def near_copy(side, m):
-        at = pl.ds(pl.multiple_of(m * H, H), H)
+        at = pl.ds(pl.multiple_of(m * Q, Q), Q)
         return pltpu.make_async_remote_copy(
             mine.at[at], gath.at[2 if side == 0 else 0, at],
             near_send.at[side, m], near_recv.at[side, m],
@@ -167,27 +168,26 @@
         return 0
 
     def shift_start(c):
-        shift_copy(2 * c).start()
-        shift_copy(2 * c + 1).start()
+        for q in (0, 2, 1, 3):
+            shift_copy(4 * c + q).start()
 
     def near_start(c):
         @pl.when(c + AHEAD < C)
         def _():
             shift_start(c + AHEAD)
 
-        shift_copy(2 * c).wait_recv()
-        near_copy(0, 2 * c).start()
-        shift_copy(2 * c + 1).wait_recv()
-        near_copy(1, 2 * c + 1).start()
-        near_copy(0, 2 * c + 1).start()
-        near_copy(1, 2 * c).start()
+        for side, q in ((0, 0), (1, 2), (0, 1), (1, 3)):
+            shift_copy(4 * c + q).wait_recv()
+            near_copy(side, 4 * c + q).start()
+        for side, q in ((0, 2), (1, 0), (0, 3), (1, 1)):
+            near_copy(side, 4 * c + q).start()
         put_halves(0, c, mine[pl.ds(pl.multiple_of(c * R, R), R), :])
 
     def forward(c):
-        near_copy(0, 2 * c).wait_recv()
-        fwd_copy(0, c).start()
-        near_copy(1, 2 * c + 1).wait_recv()
-        fwd_copy(1, c).start()
+        for side in range(2):
+            for q in range(2):
+                near_copy(side, 4 * c + 2 * side + q).wait_recv()
+            fwd_copy(side, c).start()
 
     lax.fori_loop(0, C, solve_shift, 0)
     store_solved = pltpu.make_async_copy(solved, solved_out.at[0, 0], local_sem.at[0])
@@ -286,8 +286,9 @@
             finish(c - 2)
 
         at = pl.ds(pl.multiple_of(c * R, R), R)
-        near_copy(0, 2 * c + 1).wait_recv()
-        near_copy(1, 2 * c).wait_recv()
+        for side in range(2):
+            for q in range(2):
+                near_copy(side, 4 * c + 2 * (1 - side) + q).wait_recv()
         put_halves(1, c, gath[0, at, :])
         put_halves(3, c, gath[2, at, :])
         fwd_copy(0, c).wait_recv()
@@ -326,10 +327,6 @@
         )
     ]
     stores[0].start()
-    finish(C - 1)
-    stores[1].start()
-    stores[2].start()
-
     for group in range(4):
         @pl.when(grp < GROUPS[group][2])
         def _():
@@ -354,16 +351,24 @@
             fwd_copy(side, c).wait_send()
         return 0
 
+    def drain_part(n, _):
+        part_copy(n).wait_send()
+        return 0
+
     def drain_tile(n, _):
-        part_copy(n).wait_send()
         low_copy(n).wait_send()
         high_copy(n).wait_send()
         return 0
 
-    lax.fori_loop(0, 2 * C, drain_piece, 0)
+    lax.fori_loop(0, 4 * C, drain_piece, 0)
     lax.fori_loop(0, C, drain_chunk, 0)
-    lax.fori_loop(0, TILES, drain_tile, 0)
+    lax.fori_loop(0, TILES, drain_part, 0)
+    lax.fori_loop(0, (C - 1) * (C - 1), drain_tile, 0)
     store_solved.wait()
+    finish(C - 1)
+    stores[1].start()
+    stores[2].start()
+    lax.fori_loop((C - 1) * (C - 1), TILES, drain_tile, 0)
     for store in stores:
         store.wait()
 
@@ -401,10 +406,10 @@
             dma((2,)),
             dma((4, 4)),
             dma((4, 4)),
-            dma((2 * C,)),
-            dma((2 * C,)),
-            dma((2, 2 * C)),
-            dma((2, 2 * C)),
+            dma((4 * C,)),
+            dma((4 * C,)),
+            dma((2, 4 * C)),
+            dma((2, 4 * C)),
             dma((2, C)),
             dma((2, C)),
             dma((TILES,)),

time: 150 us -> 149 us (level)
  no operation moved by 1% of the time
where the time goes in v4:
time: 149 us
  Pallas kernels  143 us (96%)
  local copies, waits for them, and re-layouts  4.78 us (3%)
    pallas_call x1, Pallas kernels, shards(): pl.pallas_call(kernel, out_shape=(block, block), in_specs=[smem] * 4 + [r...  143 us
    unnamed x4, local copies, waits for them, and re-layouts  4.78 us

profile of v4, /device:TPU:1, one launch (start us, length us, event | category | flops | bytes accessed | tf_op | source)
XLA Modules:
  0.0 148.8 jit_solution(14839118557481628752)
XLA Ops:
  1.3 142.8 %shard_map.86 = (f32[1,1,768,768]{3,2,1,0:T(8,128)}, f32[1,1,768,768]{3,2,1,0:T(8,128)}) custom-call(s32[1]{0:T(128)S(6)} %copy.11.live, s32[1,1,7]{2,1,0:T(1,128)} %first.1, s32[1,1,7]{2,1,0:T(1,128)} %second.1, s32[1,1,7]{2,1,0:T(1,128)} %offset.1, f32[1,1,768,768]{3,2,1,0:T(8,128)} %panel.1, f32[1,192,768]{2,1,0:T(8,128)} %diag.1, f32[1,1,768,768]{3,2,1,0:T(8,128)} %anc.1), custom_call_target="tpu_custom_call" | custom-call | tf_op jit(solution)/shard_map/pallas_call | solution.py:382
  144.0 0.0 copy-start
  144.0 3.4 %copy.12 = f32[1,1,768,768]{3,2,1,0:T(8,128)} copy(f32[1,1,768,768]{3,2,1,0:T(8,128)} %get-tuple-element.4) | data formatting | bytes 4718592
  147.4 0.0 copy-done
  147.4 1.4 copy.13
Async XLA Ops:
  144.0 3.4 %copy-start = (f32[1,1,768,768]{3,2,1,0:T(8,128)S(1)}, f32[1,1,768,768]{3,2,1,0:T(8,128)}, u32[]{:S(2)}) copy-start(f32[1,1,768,768]{3,2,1,0:T(8,128)} %get-tuple-element.5) | copy-start | bytes 7077892

commit v5 on v4

--- a/solution.py
+++ b/solution.py
@@ -245,6 +245,11 @@
                 preferred_element_type=jnp.float32,
             )
             terms[p] = (x[:R, :R] + (x[R:, :R] + x[:R, R:])) + x[R:, R:]
+            if p == 2:
+                @pl.when(k >= LAG)
+                def _():
+                    combine_send(n - LAG)
+
         def mix(r, _):
             at = pl.ds(pl.multiple_of(r * 16, 16), 16)
             t = [terms[p, at, :] for p in range(PAIRS)]
@@ -259,9 +264,6 @@
         lax.fori_loop(0, R // 16, mix, 0, unroll=True)
         part_copy(n).start()
 
-        @pl.when(k >= LAG)
-        def _():
-            combine_send(n - LAG)
 
     def finish(c):
         def one(k, _):

time: 149 us -> 152 us (1.020)
  Pallas kernels: 143 us -> 146 us
    pallas_call x1, Pallas kernels: 143 us -> 146 us  [shards(): pl.pallas_call(kernel, out_shape=(block, block), in_specs=[smem] * 4 + [r...]
where the time goes in v5:
time: 152 us
  Pallas kernels  146 us (96%)
  local copies, waits for them, and re-layouts  4.78 us (3%)
    pallas_call x1, Pallas kernels, shards(): pl.pallas_call(kernel, out_shape=(block, block), in_specs=[smem] * 4 + [r...  146 us
    unnamed x4, local copies, waits for them, and re-layouts  4.78 us

profile of v5, /device:TPU:1, one launch (start us, length us, event | category | flops | bytes accessed | tf_op | source)
XLA Modules:
  0.0 152.0 jit_solution(18057044822971123549)
XLA Ops:
  1.3 145.9 %shard_map.86 = (f32[1,1,768,768]{3,2,1,0:T(8,128)}, f32[1,1,768,768]{3,2,1,0:T(8,128)}) custom-call(s32[1]{0:T(128)S(6)} %copy.11.live, s32[1,1,7]{2,1,0:T(1,128)} %first.1, s32[1,1,7]{2,1,0:T(1,128)} %second.1, s32[1,1,7]{2,1,0:T(1,128)} %offset.1, f32[1,1,768,768]{3,2,1,0:T(8,128)} %panel.1, f32[1,192,768]{2,1,0:T(8,128)} %diag.1, f32[1,1,768,768]{3,2,1,0:T(8,128)} %anc.1), custom_call_target="tpu_custom_call" | custom-call | tf_op jit(solution)/shard_map/pallas_call | solution.py:384
  147.2 0.0 copy-start
  147.2 3.4 %copy.12 = f32[1,1,768,768]{3,2,1,0:T(8,128)} copy(f32[1,1,768,768]{3,2,1,0:T(8,128)} %get-tuple-element.4) | data formatting | bytes 4718592
  150.6 0.0 copy-done
  150.6 1.4 copy.13
Async XLA Ops:
  147.2 3.4 %copy-start = (f32[1,1,768,768]{3,2,1,0:T(8,128)S(1)}, f32[1,1,768,768]{3,2,1,0:T(8,128)}, u32[]{:S(2)}) copy-start(f32[1,1,768,768]{3,2,1,0:T(8,128)} %get-tuple-element.5) | copy-start | bytes 7077892
